TPU v7x, 128 devices: a whole 4x4x4 slice. The times are simulated.
128 devices in a mesh: pb: 8 (over z, core), pa: 16 (over y, x).
Axes of the slice: x: 4, y: 4, z: 4, core: 2. Of those that a mesh axis runs over, the one named last changes fastest.
Arguments:
- queries: bfloat16 [16384, 3584], P(('pb', 'pa')), may hold values from -16 to 16
- passages: bfloat16 [65536, 3584], P(('pb', 'pa')), may hold values from -16 to 16
- hard_block_offsets: int32 [4096, 4], P(('pb', 'pa')), may hold values from 0 to 126, all different within a row; in each aligned block of 32 rows (0 to 31, 32 to 63, ...) at most 2 rows name the same one
- positive: int32 [16384], P(('pb', 'pa')), may hold values from 0 to 511
- context: bfloat16 [65536, 3584], P(('pb', 'pa')), may hold values from -24 to 24
- residual: bfloat16 [65536, 3584], P(('pb', 'pa')), may hold values from -6 to 6
- output_weight: bfloat16 [3584, 3584], P(('pb', 'pa')), may hold values from -0.09375 to 0.09375
- adapter_down_weight: bfloat16 [3584, 16], replicated, may hold values from -0.09375 to 0.09375
- adapter_up_weight: bfloat16 [16, 3584], replicated, may hold values from -1.5 to 1.5
- final_norm_weight: bfloat16 [3584], replicated, may hold values from 0.099609375 to 1.8984375
Outputs:
- query_gradient: float32 [16384, 3584], P(('pb', 'pa'))
- grad_passages: float32 [65536, 3584], P(('pb', 'pa'))
- grad_lora_down: float32 [3584, 16], P(('pb', 'pa'))
- grad_lora_up: float32 [16, 3584], P(None, ('pb', 'pa'))
Inputs may be any that keep to these rules, and one draw needn't show every extreme that they name: `hard_block_offsets`: each row lists 4 different offsets. Query block k is paired with passage block (k // 32 + 1 + offset) modulo the number of devices. In each aligned block of 32 rows no offset appears more than 2 times, and some offset appears exactly 2 times.
All inputs are finite; a program needn't handle non-finite values.
Results may differ from a plain program's by a relative error of at most 0.0045.
Values may be sent and summed in bfloat16 or wider, within the bound.
A program may use at most 192 MiB of HBM per device.

v0:
```python
import math
import jax
import jax.numpy as jnp
from jax import lax
from jax.sharding import Mesh
from jax.sharding import PartitionSpec as P

MODEL_WIDTH = 3584
RERUN_QUERIES = 16
TQ = 32
PB_PA = ("pb_0", "pb_1", "pa_0", "pa_1")
CHIPS = ("pb_0", "pa_0", "pa_1")
inverse_temp = 2.0
loss_scale = 32.0
adapter_scale = 2.0
epsilon = 1e-06
absent_mass = 1e30
f32 = jnp.float32
bf16 = jnp.bfloat16


def dot(a, b, **kw):
    return jnp.dot(a, b, preferred_element_type=f32, **kw)


def two_parts(x):
    high = x.astype(bf16)
    return (high, (x - high.astype(f32)).astype(bf16))


def device_of(chip, core, per_plane):
    return chip // per_plane * 2 * per_plane + core * per_plane + chip % per_plane


def gathered_weight_input(rows):
    count = lax.axis_size(PB_PA)
    per_plane = lax.axis_size("pa_0") * lax.axis_size("pa_1")
    half = rows.shape[1] // 2
    left, right = (rows[:, :half], rows[:, half:])
    odd = lax.axis_index("pa_1") % 2 == 1
    core = lax.axis_index("pb_1")
    same = [(f, device_of(f // 2, f % 2, per_plane)) for f in range(count)]
    other = [(f, device_of(f // 2, 1 - f % 2, per_plane)) for f in range(count)]
    first = lax.ppermute(jnp.where(odd, right, left), PB_PA, same)
    second = lax.ppermute(jnp.where(odd, left, right), PB_PA, other)
    low = jnp.where(core == 0, first, second)
    high = jnp.where(core == 0, second, first)
    return jnp.concatenate([low, high], axis=0)


def exchange(array):
    return lax.all_to_all(array, PB_PA, split_axis=0, concat_axis=0, tiled=True)


def local(
    queries,
    passages,
    hard_block_offsets,
    positive,
    context,
    residual,
    output_weight,
    adapter_down_weight,
    adapter_up_weight,
    final_norm_weight,
):
    device_count = lax.axis_size(PB_PA)
    block_count, hard_count = hard_block_offsets.shape
    query_count = queries.shape[0]
    block_rows = query_count // block_count
    capacity = 2 * block_count * hard_count // device_count
    slot_rows = capacity * block_rows
    all_rows = device_count * slot_rows
    passage_count = passages.shape[0]
    score_scale = inverse_temp / math.sqrt(MODEL_WIDTH)
    weight_rows = gathered_weight_input(output_weight)
    source = lax.axis_index(PB_PA)
    target = ((source + 1 + hard_block_offsets) % device_count).reshape(-1)
    order = jnp.arange(target.shape[0], dtype=jnp.int32)
    earlier = (target[:, None] == target[None, :]) & (order[:, None] > order[None, :])
    slot = target * capacity + jnp.sum(earlier.astype(jnp.int32), axis=1)
    slot_of = slot.reshape(block_count, hard_count).T
    key = (
        jnp.repeat(slot_of, block_rows, axis=1) * block_rows
        + jnp.arange(query_count, dtype=jnp.int32) % block_rows
    )
    row_ids = jnp.arange(all_rows, dtype=jnp.int32)
    picks = row_ids[:, None] == key[0][None, :]
    for t in range(1, hard_count):
        picks = picks | (row_ids[:, None] == key[t][None, :])
    outgoing = jnp.dot(picks.astype(bf16), queries, preferred_element_type=bf16)
    arrived = exchange(outgoing.reshape(device_count, slot_rows, MODEL_WIDTH))
    arrived = arrived.reshape(-1, MODEL_WIDTH)
    half_weight = lax.all_gather(weight_rows, CHIPS, axis=0, tiled=True)
    near_scores = dot(queries, passages.T) * score_scale
    near_peak = jnp.max(near_scores, axis=1)
    near_exp = jnp.exp(near_scores - near_peak[:, None])
    near_sum = jnp.sum(near_exp, axis=1)
    near_mass = near_peak + jnp.log(near_sum)
    positive_hot = positive[:, None] == jnp.arange(passage_count, dtype=jnp.int32)[None, :]
    stacked = dot(
        jnp.concatenate([near_exp.astype(bf16), positive_hot.astype(bf16)], axis=0), passages
    )
    far_scores = dot(arrived, passages.T) * score_scale
    far_peak = jnp.max(far_scores, axis=1)
    far_exp = jnp.exp(far_scores - far_peak[:, None])
    far_sum = jnp.sum(far_exp, axis=1)
    far_mass = far_peak + jnp.log(far_sum)
    far_mean = (dot(far_exp.astype(bf16), passages) / far_sum[:, None]).astype(bf16)
    returned = exchange(far_mean.reshape(device_count, slot_rows, MODEL_WIDTH))
    returned = returned.reshape(-1, MODEL_WIDTH)
    far_mass, _ = lax.optimization_barrier((far_mass, far_mean))
    returned_mass = exchange(far_mass.reshape(device_count, slot_rows)).reshape(-1)
    half_weight, returned_mass = lax.optimization_barrier((half_weight, returned_mass))
    both_halves = lax.all_gather(half_weight, "pb_1", axis=0, tiled=False)
    hits = [key[t][:, None] == row_ids[None, :] for t in range(hard_count)]
    masses = [near_mass] + [
        jnp.sum(jnp.where(hit, returned_mass[None, :], 0.0), axis=1) for hit in hits
    ]
    peak = masses[0]
    for mass in masses[1:]:
        peak = jnp.maximum(peak, mass)
    total = jnp.exp(masses[0] - peak)
    for mass in masses[1:]:
        total = total + jnp.exp(mass - peak)
    log_total = peak + jnp.log(total)
    filled = jnp.any(picks, axis=1)
    log_outgoing = jnp.where(
        filled, jnp.sum(jnp.where(picks, log_total[None, :], 0.0), axis=1), absent_mass
    )
    log_arrived = exchange(log_outgoing.reshape(device_count, slot_rows)).reshape(-1)
    mix = jnp.zeros((query_count, all_rows), f32)
    for t in range(hard_count):
        mix = jnp.where(hits[t], jnp.exp(masses[1 + t] - log_total)[:, None], mix)
    mix_parts = jnp.concatenate(two_parts(mix), axis=0)
    near_share = jnp.exp(near_mass - log_total)
    near_part = (near_share / near_sum)[:, None] * stacked[:query_count] - stacked[query_count:]
    product_dims = (((0,), (0,)), ((), ()))
    far_weight = jnp.exp(far_scores - log_arrived[:, None]).astype(bf16)
    near_weight = (jnp.exp(near_scores - log_total[:, None]) - positive_hot.astype(f32)).astype(
        bf16
    )
    far_grad = lax.dot_general(far_weight, arrived, product_dims, preferred_element_type=f32)
    near_grad = lax.dot_general(near_weight, queries, product_dims, preferred_element_type=f32)
    grad_passages = loss_scale * score_scale * (far_grad + near_grad)
    narrow = dot(context, adapter_down_weight).astype(bf16)
    frozen = jnp.concatenate([dot(context, both_halves[0]), dot(context, both_halves[1])], axis=1)
    hidden = residual.astype(f32) + frozen + adapter_scale * dot(narrow, adapter_up_weight)
    inverse_rms = lax.rsqrt(jnp.mean(hidden * hidden, axis=1, keepdims=True) + epsilon)
    hidden_low = hidden.astype(bf16)
    hidden_up = dot(hidden_low, adapter_up_weight.T)
    token_query = jnp.arange(context.shape[0], dtype=jnp.int32) // TQ
    of_query = token_query[:, None] == jnp.arange(RERUN_QUERIES, dtype=jnp.int32)[None, :]
    narrow_sums = jnp.sum((inverse_rms * narrow.astype(f32)).reshape(RERUN_QUERIES, TQ, -1), axis=1)
    returned, hidden_low, hidden_up, inverse_rms, narrow_sums = lax.optimization_barrier(
        (returned, hidden_low, hidden_up, inverse_rms, narrow_sums)
    )
    far_part = dot(mix_parts, returned)
    query_gradient = (
        loss_scale * score_scale * (far_part[:query_count] + far_part[query_count:] + near_part)
    )
    scaled = final_norm_weight.astype(f32)[None, :] * (query_gradient[:RERUN_QUERIES] / TQ)
    products = dot(hidden_low, scaled.astype(bf16).T)
    mean = jnp.sum(jnp.where(of_query, products, 0.0), axis=1, keepdims=True) / MODEL_WIDTH
    slope = inverse_rms**3 * mean
    scaled_up = dot(scaled, adapter_up_weight.astype(f32).T, precision=lax.Precision.HIGHEST)
    spread_up = jnp.broadcast_to(
        scaled_up[:, None, :], (RERUN_QUERIES, TQ, scaled_up.shape[1])
    ).reshape(context.shape[0], -1)
    grad_narrow = (adapter_scale * (inverse_rms * spread_up - slope * hidden_up)).astype(bf16)
    down_term = lax.dot_general(grad_narrow, context, product_dims, preferred_element_type=f32)
    weighted = (slope * narrow.astype(f32)).astype(bf16)
    up_term = adapter_scale * (
        lax.dot_general(
            narrow_sums,
            scaled,
            product_dims,
            precision=lax.Precision.HIGHEST,
            preferred_element_type=f32,
        )
        - lax.dot_general(weighted, hidden_low, product_dims, preferred_element_type=f32)
    )
    terms = jnp.concatenate([down_term, up_term], axis=0) / RERUN_QUERIES
    rank = narrow.shape[1]
    columns = MODEL_WIDTH // device_count
    pieces = jnp.transpose(terms.reshape(2 * rank, device_count, columns), (1, 0, 2))
    sums = jnp.sum(exchange(pieces.reshape(device_count, -1)), axis=0).reshape(2 * rank, columns)
    return (query_gradient, grad_passages, sums[:rank].T, sums[rank:])


def solution(mesh):
    torus = Mesh(mesh.devices.reshape(4, 2, 4, 4), PB_PA)
    in_specs = (
        P(PB_PA, None),
        P(PB_PA, None),
        P(PB_PA, None),
        P(PB_PA),
        P(PB_PA, None),
        P(PB_PA, None),
        P(PB_PA, None),
        P(),
        P(),
        P(),
    )
    out_specs = (P(PB_PA, None), P(PB_PA, None), P(PB_PA, None), P(None, PB_PA))
    return jax.shard_map(local, mesh=torus, in_specs=in_specs, out_specs=out_specs, check_vma=False)
```

profile of v0, /device:TPU:1, one launch (start us, length us, event | category | flops | bytes accessed | tf_op | source)
XLA Modules:
  0.0 347.3 jit_solution(11407724801208197337)
XLA Ops:
  7.2 1.0 broadcast_select_fusion.1
  8.3 6.2 %collective-permute-start = (bf16[28,1792]{1,0:T(8,128)(2,1)S(1)}, bf16[28,1792]{1,0:T(8,128)(2,1)S(1)}, u32[]{:S(2)}, u32[]{:S(2)}) collective-permute-start(bf16[28,1792]{1,0:T(8,128)(2,1)S(1)} %get-tuple-element.32), channel_id=1, source_target_pairs={{0,0},{1,16},{2,1},{3,17},{4,2},{5,18},{6,3},{7,19},{8,4},{9,20},{... | collective-permute-start | bytes 301064 | tf_op jit(solution)/shard_map/ppermute | solution.py:44
  14.5 1.1 collective-permute-start.1
  15.6 3.1 collective-permute-done
  18.7 1.2 collective-permute-done.1
  19.9 0.7 pad_maximum_fusion
  20.7 0.8 copy.36
  22.3 2.1 convolution_bitcast_fusion
  24.3 109.4 %all_to_all.34 = bf16[128,8,3584]{2,1,0:T(8,128)(2,1)S(1)} all-to-all(bf16[128,8,3584]{2,1,0:T(8,128)(2,1)S(1)} %convolution_bitcast_fusion), channel_id=1, replica_groups=mesh['pb_0'=4,'pb_1'=2,'pa_0'=4,'pa_1'=4] {'pb_0','pb_1','pa_0','pa_1'}, dimensions={0} | all-to-all | bytes 14680064 | tf_op jit(solution)/shard_map/all_to_all | solution.py:52
  133.8 4.0 %multiply_reduce_fusion.1 = (f32[1024]{0:T(1024)S(1)}, f32[1024,512]{0,1:T(8,128)S(1)}) fusion(bf16[512,3584]{1,0:T(8,128)(2,1)S(1)} %copy-done.2, bf16[128,8,3584]{2,1,0:T(8,128)(2,1)S(1)} %all_to_all.34), kind=kOutput, calls=%fused_computation.27 | convolution fusion | flops 3759143936 | bytes 13111296 | tf_op jit(solution)/shard_map/dot_general | solution.py:23
  137.8 0.4 fusion.17
  138.2 1.0 copy-done.9
  139.1 6.1 %divide_convert_fusion = bf16[1024,3584]{1,0:T(8,128)(2,1)} fusion(f32[1024]{0:T(1024)S(1)} %fusion.17, bf16[512,3584]{1,0:T(8,128)(2,1)S(1)} %copy-done.2, f32[1024,512]{0,1:T(8,128)S(1)} %get-tuple-element.47, f32[1024]{0:T(1024)S(1)} %get-tuple-element.46), kind=kOutput, calls=%fused_computation | convolution fusion | flops 3767009280 | bytes 13115392 | tf_op jit(solution)/shard_map/dot_general | solution.py:23
  145.3 17.4 %all_to_all.35 = f32[128,1,8]{2,1,0:T(1,128)S(1)} all-to-all(f32[128,1,8]{2,1,0:T(1,128)S(1)} %bitcast.62), channel_id=1, replica_groups=mesh['pb_0'=4,'pb_1'=2,'pa_0'=4,'pa_1'=4] {'pb_0','pb_1','pa_0','pa_1'}, dimensions={0} | all-to-all | bytes 8192 | tf_op jit(solution)/shard_map/all_to_all | solution.py:52
  162.7 0.5 broadcast.136
  163.2 0.8 reduce.7
  164.1 16.1 %all-gather.4.cloned.1.call-done = bf16[3584,1792]{1,0:T(8,128)(2,1)} async-done(((bf16[56,1792]{1,0:T(8,128)(2,1)}), bf16[3584,1792]{1,0:T(8,128)(2,1)}) %all-gather.4.cloned.1.call-update) | async-done | bytes 12845072 | tf_op jit(solution)/shard_map/all_gather | solution.py:94
  180.6 3.4 fusion.72
  184.2 0.4 select_reduce_fusion.2
  185.0 17.2 %all_to_all.36 = f32[128,1,8]{2,1,0:T(1,128)S(1)} all-to-all(f32[128,1,8]{2,1,0:T(1,128)S(1)} %bitcast.63), channel_id=1, replica_groups=mesh['pb_0'=4,'pb_1'=2,'pa_0'=4,'pa_1'=4] {'pb_0','pb_1','pa_0','pa_1'}, dimensions={0} | all-to-all | bytes 8192 | tf_op jit(solution)/shard_map/all_to_all | solution.py:52
  202.3 5.9 %all-to-all-start.2 = ((bf16[128,8,3584]{2,1,0:T(8,128)(2,1)}), bf16[128,8,3584]{2,1,0:T(8,128)(2,1)}, u32[]{:S(2)}, u32[]{:S(2)}) async-start(bf16[128,8,3584]{2,1,0:T(8,128)(2,1)} %bitcast.61), calls=%async_computation.2 | async-start | bytes 14680064 | tf_op jit(solution)/shard_map/all_to_all | solution.py:52
  208.2 6.3 %copy.39 = bf16[512,3584]{0,1:T(8,128)(2,1)} copy(bf16[512,3584]{1,0:T(8,128)(2,1)} %param.15) | data formatting | bytes 7340032 | tf_op args[5]
  214.6 3.2 convolution_convert_fusion
  217.8 3.1 fusion.35
  221.6 0.8 reduce.8
  222.5 10.6 %fusion.5 = f32[512,3584]{1,0:T(8,128)} fusion(bf16[128,8,3584]{2,1,0:T(8,128)(2,1)} %copy-done.6, f32[1024,512]{0,1:T(8,128)} %copy-done.9, f32[1024]{0:T(1024)S(1)} %sub.236), kind=kOutput, calls=%fused_computation.7 | convolution fusion | flops 3759669248 | bytes 16781312 | tf_op jit(solution)/shard_map/dot_general | solution.py:143
  233.1 12.7 %fusion.10 = f32[512,1792]{0,1:T(8,128)S(1)} fusion(bf16[512,3584]{1,0:T(8,128)(2,1)} %param.14, bf16[7168,1792]{1,0:T(8,128)(2,1)} %all-gather.6.cloned.1.call-done), kind=kOutput, calls=%fused_computation.16 | convolution fusion | flops 6576668672 | bytes 20185088 | tf_op jit(solution)/shard_map/dot_general | solution.py:23
  245.8 10.3 %fusion.13 = f32[512,1792]{0,1:T(8,128)S(1)} fusion(bf16[512,3584]{1,0:T(8,128)(2,1)S(1)} %copy-done.4, bf16[7168,1792]{1,0:T(8,128)(2,1)} %all-gather.6.cloned.1.call-done), kind=kOutput, calls=%fused_computation.17 | convolution fusion | flops 6576668672 | bytes 20185088 | tf_op jit(solution)/shard_map/dot_general | solution.py:23
  256.2 3.6 %multiply_reduce_fusion = (f32[512]{0:T(512)S(1)}, bf16[512,3584]{0,1:T(8,128)(2,1)}) fusion(bf16[512,16]{0,1:T(8,128)(2,1)S(1)} %convolution_convert_fusion, bf16[16,3584]{1,0:T(8,128)(2,1)S(1)} %copy-done.10, f32[512,1792]{0,1:T(8,128)S(1)} %fusion.13, f32[512,1792]{0,1:T(8,128)S(1)} %fusion.10, bf16[512,3584]{0,1:T(8,128)(2,1)S(1)} %copy-done.7), kind=kOutput, calls=%fused_computation.12 | convolution fusion | flops 73399808 | bytes 14813184 | tf_op jit(solution)/shard_map/dot_general | solution.py:23
  260.0 2.6 fusion.73
  262.6 32.0 %all-to-all-done.2 = bf16[128,8,3584]{2,1,0:T(8,128)(2,1)} async-done(((bf16[128,8,3584]{2,1,0:T(8,128)(2,1)}), bf16[128,8,3584]{2,1,0:T(8,128)(2,1)}, u32[]{:S(2)}, u32[]{:S(2)}) %all-to-all-start.2) | async-done | bytes 7340064 | tf_op jit(solution)/shard_map/all_to_all | solution.py:52
  294.6 5.3 %fusion.26 = f32[256,3584]{1,0:T(8,128)S(1)} fusion(bf16[1024,3584]{1,0:T(8,128)(2,1)} %bitcast.9, bf16[128,1024]{1,0:T(8,128)(2,1)S(1)} %subtract_convert_fusion, bf16[128,1024]{1,0:T(8,128)(2,1)S(1)} %fusion.30), kind=kOutput, calls=%fused_computation.36 | convolution fusion | flops 1880096768 | bytes 11534336 | tf_op jit(solution)/shard_map/dot_general | solution.py:23
  299.9 0.6 fusion.19
  300.7 1.8 copy-done.1
  302.6 0.6 fusion.20
  303.4 2.6 fusion.54
  306.0 1.3 concatenate.24
  307.3 0.4 copy.43
  307.7 1.3 fusion.42
  309.0 3.1 fusion.9
  312.1 1.3 concatenate.25
  313.4 0.4 copy.44
  314.1 1.3 copy.46
  315.4 10.0 %all-to-all-start.4 = ((f32[128,1,896]{2,1,0:T(1,128)}), f32[128,1,896]{2,1,0:T(1,128)S(1)}, u32[]{:S(2)}, u32[]{:S(2)}) async-start(f32[128,1,896]{2,1,0:T(1,128)} %copy.46), calls=%async_computation.4 | async-start | bytes 917504 | tf_op jit(solution)/shard_map/all_to_all | solution.py:52
  325.4 7.4 %add_multiply_fusion = f32[512,3584]{1,0:T(8,128)} fusion(f32[512,3584]{1,0:T(8,128)} %fusion.5, bf16[128,3584]{1,0:T(8,128)(2,1)S(1)} %copy-done, f32[128,512]{1,0:T(8,128)S(1)} %get-tuple-element.45, f32[128]{0:T(128)S(1)} %get-tuple-element.25, s32[128]{0:T(128)S(1)} %copy-done.13), kind=kOutput, calls=%fused_computation.11 | convolution fusion | flops 473759744 | bytes 15860736 | tf_op jit(solution)/shard_map/dot_general | solution.py:144
  332.8 5.9 %all-to-all-done.4 = f32[128,1,896]{2,1,0:T(1,128)S(1)} async-done(((f32[128,1,896]{2,1,0:T(1,128)}), f32[128,1,896]{2,1,0:T(1,128)S(1)}, u32[]{:S(2)}, u32[]{:S(2)}) %all-to-all-start.4) | async-done | bytes 458784 | tf_op jit(solution)/shard_map/all_to_all | solution.py:52
  339.1 0.7 slice.85
  339.8 0.7 slice.87
  (73 shorter events, 4.2 us)
Async XLA Ops:
  7.2 15.1 %copy-start = (bf16[128,3584]{1,0:T(8,128)(2,1)S(1)}, bf16[128,3584]{1,0:T(8,128)(2,1)}, u32[]{:S(2)}) copy-start(bf16[128,3584]{1,0:T(8,128)(2,1)} %param.10) | copy-start | bytes 2752516
  7.2 173.1 %all-gather.4.cloned.1.call-start = ((), (), s32[]{:S(2)}) async-start(), calls=%async_computation.5 | async-start | bytes 13045760 | tf_op jit(solution)/shard_map/all_gather | solution.py:94
  8.3 10.4 %collective-permute-start = (bf16[28,1792]{1,0:T(8,128)(2,1)S(1)}, bf16[28,1792]{1,0:T(8,128)(2,1)S(1)}, u32[]{:S(2)}, u32[]{:S(2)}) collective-permute-start(bf16[28,1792]{1,0:T(8,128)(2,1)S(1)} %get-tuple-element.32), channel_id=1, source_target_pairs={{0,0},{1,16},{2,1},{3,17},{4,2},{5,18},{6,3},{7,19},{8,4},{9,20},{... | collective-permute-start | bytes 301064 | tf_op jit(solution)/shard_map/ppermute | solution.py:44
  14.5 5.4 %collective-permute-start.1 = (bf16[28,1792]{1,0:T(8,128)(2,1)S(1)}, bf16[28,1792]{1,0:T(8,128)(2,1)S(1)}, u32[]{:S(2)}, u32[]{:S(2)}) collective-permute-start(bf16[28,1792]{1,0:T(8,128)(2,1)S(1)} %get-tuple-element.33), channel_id=1, source_target_pairs={{0,16},{1,0},{2,17},{3,1},{4,18},{5,2},{6,19},{7,3},{8,20},{9,4},{... | collective-permute-start | bytes 301064 | tf_op jit(solution)/shard_map/ppermute | solution.py:45
  20.7 212.4 %all-gather.6.cloned.1.call-start = ((), (), s32[]{:S(2)}) async-start(), calls=%async_computation.6 | async-start | bytes 38535168 | tf_op jit(solution)/shard_map/all_gather | solution.py:115
  24.3 109.4 %copy-start.2 = (bf16[512,3584]{1,0:T(8,128)(2,1)S(1)}, bf16[512,3584]{1,0:T(8,128)(2,1)}, u32[]{:S(2)}) copy-start(bf16[512,3584]{1,0:T(8,128)(2,1)} %param.11) | copy-start | bytes 11010052
  133.8 4.0 %copy-start.6 = (bf16[128,8,3584]{2,1,0:T(8,128)(2,1)}, bf16[128,8,3584]{2,1,0:T(8,128)(2,1)S(1)}, u32[]{:S(2)}) copy-start(bf16[128,8,3584]{2,1,0:T(8,128)(2,1)S(1)} %all_to_all.34) | copy-start | bytes 22020100
  137.8 1.4 copy-start.9
  202.3 5.9 %copy-start.12 = (bf16[3584]{0:T(1024)(128)(2,1)S(1)}, bf16[3584]{0:T(1024)(128)(2,1)}, u32[]{:S(2)}) copy-start(bf16[3584]{0:T(1024)(128)(2,1)} %param.19) | copy-start | bytes 21508
  202.3 92.3 %all-to-all-start.2 = ((bf16[128,8,3584]{2,1,0:T(8,128)(2,1)}), bf16[128,8,3584]{2,1,0:T(8,128)(2,1)}, u32[]{:S(2)}, u32[]{:S(2)}) async-start(bf16[128,8,3584]{2,1,0:T(8,128)(2,1)} %bitcast.61), calls=%async_computation.2 | async-start | bytes 14680064 | tf_op jit(solution)/shard_map/all_to_all | solution.py:52
  208.1 6.4 %copy-start.13 = (s32[128]{0:T(128)S(1)}, s32[128]{0:T(128)}, u32[]{:S(2)}) copy-start(s32[128]{0:T(128)} %param.13) | copy-start | bytes 1540
  208.2 6.4 %copy-start.11 = (bf16[3584,16]{0,1:T(8,128)(2,1)S(1)}, bf16[3584,16]{0,1:T(8,128)(2,1)}, u32[]{:S(2)}) copy-start(bf16[3584,16]{0,1:T(8,128)(2,1)} %param.17) | copy-start | bytes 344068
  214.5 3.3 copy-start.3
  233.1 12.7 %copy-start.4 = (bf16[512,3584]{1,0:T(8,128)(2,1)S(1)}, bf16[512,3584]{1,0:T(8,128)(2,1)}, u32[]{:S(2)}) copy-start(bf16[512,3584]{1,0:T(8,128)(2,1)} %param.14) | copy-start | bytes 11010052
  245.8 10.4 %copy-start.7 = (bf16[512,3584]{0,1:T(8,128)(2,1)S(1)}, bf16[512,3584]{0,1:T(8,128)(2,1)}, u32[]{:S(2)}) copy-start(bf16[512,3584]{0,1:T(8,128)(2,1)} %copy.39) | copy-start | bytes 11010052
  245.8 10.4 %copy-start.10 = (bf16[16,3584]{1,0:T(8,128)(2,1)S(1)}, bf16[16,3584]{1,0:T(8,128)(2,1)}, u32[]{:S(2)}) copy-start(bf16[16,3584]{1,0:T(8,128)(2,1)} %param.18) | copy-start | bytes 344068
  294.6 5.3 %copy-start.5 = (f32[256,3584]{1,0:T(8,128)S(1)}, f32[256,3584]{1,0:T(8,128)}, u32[]{:S(2)}) copy-start(f32[256,3584]{1,0:T(8,128)} %fusion.35) | copy-start | bytes 11010052
  299.9 2.7 copy-start.1
  300.5 2.7 copy-start.8
  315.4 23.3 %all-to-all-start.4 = ((f32[128,1,896]{2,1,0:T(1,128)}), f32[128,1,896]{2,1,0:T(1,128)S(1)}, u32[]{:S(2)}, u32[]{:S(2)}) async-start(f32[128,1,896]{2,1,0:T(1,128)} %copy.46), calls=%async_computation.4 | async-start | bytes 917504 | tf_op jit(solution)/shard_map/all_to_all | solution.py:52
Sparse Core Ops, SparseCore 0:
  20.8 159.4 all-gather.3
  181.9 45.9 all-gather.5
where the time goes:
time: 348 us; the launch traced here: 347 us
  blocking collectives  144 us (41%)
  matrix products  82.2 us (24%)
  waiting for transfers between devices  58.3 us (17%)
  starting transfers between devices  23.3 us (7%)
  local copies, waits for them, and re-layouts  18 us (5%)
  between operations  14.5 us (4%)
  other arithmetic  6.98 us (2%)
    all_to_all x3, blocking collectives, exchange(): return lax.all_to_all(array, PB_PA, split_axis=0, concat_axis=0, tiled=True)  144 us
    dot_general x12, matrix products, dot(): return jnp.dot(a, b, preferred_element_type=f32, **kw)  55.1 us
    all_to_all x2, waiting for transfers between devices, exchange(): return lax.all_to_all(array, PB_PA, split_axis=0, concat_axis=0, tiled=True)  37.9 us
    all_gather x1, waiting for transfers between devices, local(): half_weight = lax.all_gather(weight_rows, CHIPS, axis=0, tiled=True)  16.1 us
    all_to_all x2, starting transfers between devices, exchange(): return lax.all_to_all(array, PB_PA, split_axis=0, concat_axis=0, tiled=True)  15.9 us
    dot_general x1, matrix products, local(): lax.dot_general(far_weight, arrived, product_dims, preferred_element_type...  10.6 us
    unnamed x30, local copies, waits for them, and re-layouts  9.97 us
    dot_general x1, matrix products, local(): lax.dot_general(near_weight, queries, product_dims, preferred_element_typ...  7.38 us
  transfers between devices with their start and end apart: 6, of which 5 were waited for; matrix products, arithmetic and copies ran while one was open for 24% of the time, Pallas kernels for 0%

commit v1 on v0

--- a/solution.py
+++ b/solution.py
@@ -91,7 +91,10 @@
     outgoing = jnp.dot(picks.astype(bf16), queries, preferred_element_type=bf16)
     arrived = exchange(outgoing.reshape(device_count, slot_rows, MODEL_WIDTH))
     arrived = arrived.reshape(-1, MODEL_WIDTH)
-    half_weight = lax.all_gather(weight_rows, CHIPS, axis=0, tiled=True)
+    size = lax.axis_size(CHIPS)
+    parts = jnp.stack([weight_rows for _ in range(size)])
+    parts = lax.all_to_all(parts, CHIPS, split_axis=0, concat_axis=0)
+    half_weight = jnp.concatenate(parts, axis=0)
     near_scores = dot(queries, passages.T) * score_scale
     near_peak = jnp.max(near_scores, axis=1)
     near_exp = jnp.exp(near_scores - near_peak[:, None])

time: 348 us -> 547 us (1.57)
  waiting for transfers between devices: 58.3 us -> 338 us
  blocking collectives: 144 us -> 18.8 us
  starting transfers between devices: 23.3 us -> 56.2 us
  matrix products: 82.2 us -> 89.3 us
  local copies, waits for them, and re-layouts: 18 us -> 24.2 us
    all_to_all x0 -> x1, waiting for transfers between devices: none -> 210 us  [local(): parts = lax.all_to_all(parts, CHIPS, split_axis=0, concat_axis=0)]
    all_to_all x3 -> x1, blocking collectives: 144 us -> 18.8 us  [exchange(): return lax.all_to_all(array, PB_PA, split_axis=0, concat_axis=0, tiled=True)]
    ppermute x1, waiting for transfers between devices: 3.09 us -> 79 us  [gathered_weight_input(): first = lax.ppermute(jnp.where(odd, right, left), PB_PA, same)]
    all_to_all x2 -> x4, starting transfers between devices: 15.9 us -> 44.3 us  [exchange(): return lax.all_to_all(array, PB_PA, split_axis=0, concat_axis=0, tiled=True)]
    all_gather x1 -> x0, waiting for transfers between devices: 16.1 us -> none  [local(): half_weight = lax.all_gather(weight_rows, CHIPS, axis=0, tiled=True)]
    all_to_all x2 -> x4, waiting for transfers between devices: 37.9 us -> 48.8 us  [exchange(): return lax.all_to_all(array, PB_PA, split_axis=0, concat_axis=0, tiled=True)]
    all_to_all x0 -> x1, starting transfers between devices: none -> 5.79 us  [local(): parts = lax.all_to_all(parts, CHIPS, split_axis=0, concat_axis=0)]
  transfers between devices with their start and end apart: 6 -> 8, of which waited for: 5 -> 6; matrix products, arithmetic and copies ran while one was open for 24% -> 12% of each run, Pallas kernels for 0% -> 0%
where the time goes in v1:
time: 547 us; the launch traced here: 546 us
  waiting for transfers between devices  338 us (62%)
  matrix products  89.3 us (16%)
  starting transfers between devices  56.2 us (10%)
  local copies, waits for them, and re-layouts  24.2 us (4%)
  blocking collectives  18.8 us (3%)
  between operations  14.5 us (3%)
    all_to_all x1, waiting for transfers between devices, local(): parts = lax.all_to_all(parts, CHIPS, split_axis=0, concat_axis=0)  210 us
    ppermute x1, waiting for transfers between devices, gathered_weight_input(): first = lax.ppermute(jnp.where(odd, right, left), PB_PA, same)  79 us
    dot_general x12, matrix products, dot(): return jnp.dot(a, b, preferred_element_type=f32, **kw)  59.3 us
    all_to_all x4, waiting for transfers between devices, exchange(): return lax.all_to_all(array, PB_PA, split_axis=0, concat_axis=0, tiled=True)  48.8 us
    all_to_all x4, starting transfers between devices, exchange(): return lax.all_to_all(array, PB_PA, split_axis=0, concat_axis=0, tiled=True)  44.3 us
    all_to_all x1, blocking collectives, exchange(): return lax.all_to_all(array, PB_PA, split_axis=0, concat_axis=0, tiled=True)  18.8 us
  transfers between devices with their start and end apart: 8, of which 6 were waited for; matrix products, arithmetic and copies ran while one was open for 12% of the time, Pallas kernels for 0%

profile of v1, /device:TPU:1, one launch (start us, length us, event | category | flops | bytes accessed | tf_op | source)
XLA Modules:
  0.0 545.9 jit_solution(11081262769690346727)
XLA Ops:
  7.2 0.8 copy.36
  8.8 5.1 convolution_bitcast_fusion
  13.9 11.9 %all-to-all-start.1 = ((bf16[128,8,3584]{2,1,0:T(8,128)(2,1)}), bf16[128,8,3584]{2,1,0:T(8,128)(2,1)}, u32[]{:S(2)}, u32[]{:S(2)}) async-start(bf16[128,8,3584]{2,1,0:T(8,128)(2,1)} %convolution_bitcast_fusion), calls=%async_computation.1 | async-start | bytes 14680064 | tf_op jit(solution)/shard_map/all_to_all | solution.py:52
  25.9 5.1 collective-permute-start
  30.9 1.0 collective-permute-start.1
  31.9 79.0 %collective-permute-done = bf16[28,1792]{1,0:T(8,128)(2,1)S(1)} collective-permute-done((bf16[28,1792]{1,0:T(8,128)(2,1)S(1)}, bf16[28,1792]{1,0:T(8,128)(2,1)S(1)}, u32[]{:S(2)}, u32[]{:S(2)}) %collective-permute-start) | collective-permute-done | bytes 100384 | tf_op jit(solution)/shard_map/ppermute | solution.py:44
  111.0 1.5 all-to-all-done.1
  112.5 8.1 %multiply_reduce_fusion.1 = (f32[1024]{0:T(1024)S(1)}, f32[1024,512]{0,1:T(8,128)S(1)}) fusion(bf16[512,3584]{1,0:T(8,128)(2,1)} %param.11, bf16[128,8,3584]{2,1,0:T(8,128)(2,1)} %all-to-all-done.1), kind=kOutput, calls=%fused_computation.27 | convolution fusion | flops 3759143936 | bytes 13111296 | tf_op jit(solution)/shard_map/dot_general | solution.py:23
  120.7 0.4 fusion.17
  121.1 1.0 copy-done.8
  122.0 6.1 %divide_convert_fusion = bf16[1024,3584]{1,0:T(8,128)(2,1)} fusion(f32[1024]{0:T(1024)S(1)} %fusion.17, bf16[512,3584]{1,0:T(8,128)(2,1)S(1)} %copy-done.2, f32[1024,512]{0,1:T(8,128)S(1)} %get-tuple-element.47, f32[1024]{0:T(1024)S(1)} %get-tuple-element.46), kind=kOutput, calls=%fused_computation | convolution fusion | flops 3767009280 | bytes 13115392 | tf_op jit(solution)/shard_map/dot_general | solution.py:23
  128.1 0.7 all_to_all.27
  128.9 16.6 %all-to-all-start.2 = ((f32[128,1,8]{2,1,0:T(1,128)}), f32[128,1,8]{2,1,0:T(1,128)S(1)}, u32[]{:S(2)}, u32[]{:S(2)}) async-start(f32[128,1,8]{2,1,0:T(1,128)} %bitcast.8), calls=%async_computation.2 | async-start | bytes 131072 | tf_op jit(solution)/shard_map/all_to_all | solution.py:52
  145.6 9.5 %all-to-all-done.2 = f32[128,1,8]{2,1,0:T(1,128)S(1)} async-done(((f32[128,1,8]{2,1,0:T(1,128)}), f32[128,1,8]{2,1,0:T(1,128)S(1)}, u32[]{:S(2)}, u32[]{:S(2)}) %all-to-all-start.2) | async-done | bytes 4128 | tf_op jit(solution)/shard_map/all_to_all | solution.py:52
  155.0 5.4 stack.2
  160.4 5.8 %all-to-all-start = ((bf16[64,56,1792]{2,1,0:T(8,128)(2,1)}), bf16[64,56,1792]{2,1,0:T(8,128)(2,1)}, u32[]{:S(2)}, u32[]{:S(2)}) async-start(bf16[64,56,1792]{2,1,0:T(8,128)(2,1)} %stack.2), calls=%async_computation | async-start | bytes 25690112 | tf_op jit(solution)/shard_map/all_to_all | solution.py:96
  166.3 0.5 broadcast.138
  166.8 0.8 reduce.7
  167.7 209.8 %all-to-all-done = bf16[64,56,1792]{2,1,0:T(8,128)(2,1)} async-done(((bf16[64,56,1792]{2,1,0:T(8,128)(2,1)}), bf16[64,56,1792]{2,1,0:T(8,128)(2,1)}, u32[]{:S(2)}, u32[]{:S(2)}) %all-to-all-start) | async-done | bytes 12845088 | tf_op jit(solution)/shard_map/all_to_all | solution.py:96
  377.8 3.4 fusion.72
  381.4 0.4 select_reduce_fusion.2
  382.2 18.8 %all_to_all.39 = f32[128,1,8]{2,1,0:T(1,128)S(1)} all-to-all(f32[128,1,8]{2,1,0:T(1,128)S(1)} %bitcast.63), channel_id=1, replica_groups=mesh['pb_0'=4,'pb_1'=2,'pa_0'=4,'pa_1'=4] {'pb_0','pb_1','pa_0','pa_1'}, dimensions={0} | all-to-all | bytes 8192 | tf_op jit(solution)/shard_map/all_to_all | solution.py:52
  401.0 5.7 %all-to-all-start.3 = ((bf16[128,8,3584]{2,1,0:T(8,128)(2,1)}), bf16[128,8,3584]{2,1,0:T(8,128)(2,1)}, u32[]{:S(2)}, u32[]{:S(2)}) async-start(bf16[128,8,3584]{2,1,0:T(8,128)(2,1)} %bitcast.62), calls=%async_computation.3 | async-start | bytes 14680064 | tf_op jit(solution)/shard_map/all_to_all | solution.py:52
  406.8 6.4 %copy.39 = bf16[512,3584]{0,1:T(8,128)(2,1)} copy(bf16[512,3584]{1,0:T(8,128)(2,1)} %param.15) | data formatting | bytes 7340032 | tf_op args[5]
  413.3 3.2 convolution_convert_fusion
  416.5 3.1 fusion.35
  420.3 0.8 reduce.8
  421.2 10.6 %fusion.5 = f32[512,3584]{1,0:T(8,128)} fusion(bf16[128,8,3584]{2,1,0:T(8,128)(2,1)} %all-to-all-done.1, f32[1024,512]{0,1:T(8,128)} %copy-done.8, f32[1024]{0:T(1024)S(1)} %sub.236), kind=kOutput, calls=%fused_computation.7 | convolution fusion | flops 3759669248 | bytes 16781312 | tf_op jit(solution)/shard_map/dot_general | solution.py:146
  431.8 12.7 %fusion.10 = f32[512,1792]{0,1:T(8,128)S(1)} fusion(bf16[512,3584]{1,0:T(8,128)(2,1)} %param.14, bf16[7168,1792]{1,0:T(8,128)(2,1)} %all-gather.3.cloned.1.call-done), kind=kOutput, calls=%fused_computation.16 | convolution fusion | flops 6576668672 | bytes 20185088 | tf_op jit(solution)/shard_map/dot_general | solution.py:23
  444.5 10.3 %fusion.13 = f32[512,1792]{0,1:T(8,128)S(1)} fusion(bf16[512,3584]{1,0:T(8,128)(2,1)S(1)} %copy-done.4, bf16[7168,1792]{1,0:T(8,128)(2,1)} %all-gather.3.cloned.1.call-done), kind=kOutput, calls=%fused_computation.17 | convolution fusion | flops 6576668672 | bytes 20185088 | tf_op jit(solution)/shard_map/dot_general | solution.py:23
  454.9 3.5 multiply_reduce_fusion
  458.7 2.6 fusion.73
  461.3 31.9 %all-to-all-done.3 = bf16[128,8,3584]{2,1,0:T(8,128)(2,1)} async-done(((bf16[128,8,3584]{2,1,0:T(8,128)(2,1)}), bf16[128,8,3584]{2,1,0:T(8,128)(2,1)}, u32[]{:S(2)}, u32[]{:S(2)}) %all-to-all-start.3) | async-done | bytes 7340064 | tf_op jit(solution)/shard_map/all_to_all | solution.py:52
  493.2 5.3 fusion.26
  498.5 0.6 fusion.19
  499.3 1.8 copy-done.1
  501.2 0.6 fusion.20
  502.0 2.6 fusion.54
  504.6 1.3 concatenate.24
  506.3 1.3 fusion.42
  507.6 3.1 fusion.9
  510.7 1.3 concatenate.25
  512.7 1.3 copy.46
  514.0 10.0 %all-to-all-start.5 = ((f32[128,1,896]{2,1,0:T(1,128)}), f32[128,1,896]{2,1,0:T(1,128)S(1)}, u32[]{:S(2)}, u32[]{:S(2)}) async-start(f32[128,1,896]{2,1,0:T(1,128)} %copy.46), calls=%async_computation.5 | async-start | bytes 917504 | tf_op jit(solution)/shard_map/all_to_all | solution.py:52
  524.0 7.4 %add_multiply_fusion = f32[512,3584]{1,0:T(8,128)} fusion(f32[512,3584]{1,0:T(8,128)} %fusion.5, bf16[128,3584]{1,0:T(8,128)(2,1)S(1)} %copy-done, f32[128,512]{1,0:T(8,128)S(1)} %get-tuple-element.45, f32[128]{0:T(128)S(1)} %get-tuple-element.25, s32[128]{0:T(128)S(1)} %copy-done.13), kind=kOutput, calls=%fused_computation.11 | convolution fusion | flops 473759744 | bytes 15860736 | tf_op jit(solution)/shard_map/dot_general | solution.py:147
  531.4 5.9 %all-to-all-done.5 = f32[128,1,896]{2,1,0:T(1,128)S(1)} async-done(((f32[128,1,896]{2,1,0:T(1,128)}), f32[128,1,896]{2,1,0:T(1,128)S(1)}, u32[]{:S(2)}, u32[]{:S(2)}) %all-to-all-start.5) | async-done | bytes 458784 | tf_op jit(solution)/shard_map/all_to_all | solution.py:52
  537.7 0.7 slice.85
  538.4 0.7 slice.87
  (75 shorter events, 4.9 us)
Async XLA Ops:
  7.2 1.6 copy-start
  13.9 11.9 %copy-start.10 = (bf16[28,3584]{1,0:T(8,128)(2,1)S(1)}, bf16[28,3584]{1,0:T(8,128)(2,1)}, u32[]{:S(2)}) copy-start(bf16[28,3584]{1,0:T(8,128)(2,1)} %param.16) | copy-start | bytes 602116
  13.9 98.6 %all-to-all-start.1 = ((bf16[128,8,3584]{2,1,0:T(8,128)(2,1)}), bf16[128,8,3584]{2,1,0:T(8,128)(2,1)}, u32[]{:S(2)}, u32[]{:S(2)}) async-start(bf16[128,8,3584]{2,1,0:T(8,128)(2,1)} %convolution_bitcast_fusion), calls=%async_computation.1 | async-start | bytes 14680064 | tf_op jit(solution)/shard_map/all_to_all | solution.py:52
  25.9 85.1 %collective-permute-start = (bf16[28,1792]{1,0:T(8,128)(2,1)S(1)}, bf16[28,1792]{1,0:T(8,128)(2,1)S(1)}, u32[]{:S(2)}, u32[]{:S(2)}) collective-permute-start(bf16[28,1792]{1,0:T(8,128)(2,1)S(1)} %get-tuple-element.32), channel_id=1, source_target_pairs={{0,0},{1,16},{2,1},{3,17},{4,2},{5,18},{6,3},{7,19},{8,4},{9,20},{... | collective-permute-start | bytes 301064 | tf_op jit(solution)/shard_map/ppermute | solution.py:44
  30.9 80.1 %collective-permute-start.1 = (bf16[28,1792]{1,0:T(8,128)(2,1)S(1)}, bf16[28,1792]{1,0:T(8,128)(2,1)S(1)}, u32[]{:S(2)}, u32[]{:S(2)}) collective-permute-start(bf16[28,1792]{1,0:T(8,128)(2,1)S(1)} %get-tuple-element.33), channel_id=1, source_target_pairs={{0,16},{1,0},{2,17},{3,1},{4,18},{5,2},{6,19},{7,3},{8,20},{9,4},{... | collective-permute-start | bytes 301064 | tf_op jit(solution)/shard_map/ppermute | solution.py:45
  112.5 9.5 %copy-start.2 = (bf16[512,3584]{1,0:T(8,128)(2,1)S(1)}, bf16[512,3584]{1,0:T(8,128)(2,1)}, u32[]{:S(2)}) copy-start(bf16[512,3584]{1,0:T(8,128)(2,1)} %param.11) | copy-start | bytes 11010052
  120.7 1.4 copy-start.8
  128.9 26.2 %all-to-all-start.2 = ((f32[128,1,8]{2,1,0:T(1,128)}), f32[128,1,8]{2,1,0:T(1,128)S(1)}, u32[]{:S(2)}, u32[]{:S(2)}) async-start(f32[128,1,8]{2,1,0:T(1,128)} %bitcast.8), calls=%async_computation.2 | async-start | bytes 131072 | tf_op jit(solution)/shard_map/all_to_all | solution.py:52
  160.4 217.1 %all-to-all-start = ((bf16[64,56,1792]{2,1,0:T(8,128)(2,1)}), bf16[64,56,1792]{2,1,0:T(8,128)(2,1)}, u32[]{:S(2)}, u32[]{:S(2)}) async-start(bf16[64,56,1792]{2,1,0:T(8,128)(2,1)} %stack.2), calls=%async_computation | async-start | bytes 25690112 | tf_op jit(solution)/shard_map/all_to_all | solution.py:96
  166.2 265.5 %all-gather.3.cloned.1.call-start = ((), (), s32[]{:S(2)}) async-start(), calls=%async_computation.6 | async-start | bytes 38535168 | tf_op jit(solution)/shard_map/all_gather | solution.py:118
  401.0 5.7 %copy-start.12 = (bf16[3584]{0:T(1024)(128)(2,1)S(1)}, bf16[3584]{0:T(1024)(128)(2,1)}, u32[]{:S(2)}) copy-start(bf16[3584]{0:T(1024)(128)(2,1)} %param.19) | copy-start | bytes 21508
  401.0 92.2 %all-to-all-start.3 = ((bf16[128,8,3584]{2,1,0:T(8,128)(2,1)}), bf16[128,8,3584]{2,1,0:T(8,128)(2,1)}, u32[]{:S(2)}, u32[]{:S(2)}) async-start(bf16[128,8,3584]{2,1,0:T(8,128)(2,1)} %bitcast.62), calls=%async_computation.3 | async-start | bytes 14680064 | tf_op jit(solution)/shard_map/all_to_all | solution.py:52
  406.7 6.5 %copy-start.13 = (s32[128]{0:T(128)S(1)}, s32[128]{0:T(128)}, u32[]{:S(2)}) copy-start(s32[128]{0:T(128)} %param.13) | copy-start | bytes 1540
  406.8 6.5 %copy-start.11 = (bf16[3584,16]{0,1:T(8,128)(2,1)S(1)}, bf16[3584,16]{0,1:T(8,128)(2,1)}, u32[]{:S(2)}) copy-start(bf16[3584,16]{0,1:T(8,128)(2,1)} %param.17) | copy-start | bytes 344068
  413.2 3.3 copy-start.3
  431.8 12.7 %copy-start.4 = (bf16[512,3584]{1,0:T(8,128)(2,1)S(1)}, bf16[512,3584]{1,0:T(8,128)(2,1)}, u32[]{:S(2)}) copy-start(bf16[512,3584]{1,0:T(8,128)(2,1)} %param.14) | copy-start | bytes 11010052
  444.5 10.4 %copy-start.6 = (bf16[512,3584]{0,1:T(8,128)(2,1)S(1)}, bf16[512,3584]{0,1:T(8,128)(2,1)}, u32[]{:S(2)}) copy-start(bf16[512,3584]{0,1:T(8,128)(2,1)} %copy.39) | copy-start | bytes 11010052
  444.5 10.4 %copy-start.9 = (bf16[16,3584]{1,0:T(8,128)(2,1)S(1)}, bf16[16,3584]{1,0:T(8,128)(2,1)}, u32[]{:S(2)}) copy-start(bf16[16,3584]{1,0:T(8,128)(2,1)} %param.18) | copy-start | bytes 344068
  493.2 5.3 copy-start.5
  498.5 2.7 copy-start.1
  499.1 2.7 copy-start.7
  514.0 23.3 %all-to-all-start.5 = ((f32[128,1,896]{2,1,0:T(1,128)}), f32[128,1,896]{2,1,0:T(1,128)S(1)}, u32[]{:S(2)}, u32[]{:S(2)}) async-start(f32[128,1,896]{2,1,0:T(1,128)} %copy.46), calls=%async_computation.5 | async-start | bytes 917504 | tf_op jit(solution)/shard_map/all_to_all | solution.py:52
Sparse Core Ops, SparseCore 0:
  377.7 47.4 all-gather.2
